TPU v7x, 512 devices: a whole 4x8x8 slice. The times are simulated.
512 devices in a mesh: wide: 64 (over x, y, core), narrow: 8 (over z).
Axes of the slice: x: 4, y: 8, z: 8, core: 2. Of those that a mesh axis runs over, the one named last changes fastest.
Arguments:
- points: bfloat16 [128, 1024, 512], P('wide', 'narrow'), may hold values from -6 to 6
- counts: int32 [128, 256], P('wide', 'narrow'), may hold values from 1 to 4, as said below
- destination: int32 [128, 256], P('wide', 'narrow'), may hold values from 0 to 63, as said below
- rotated_ball: int32 [128, 256], P('wide', 'narrow'), may hold values from 0 to 1
- qkv_first: bfloat16 [512, 1536], replicated, may hold values from -1 to 1
- out_first: bfloat16 [512, 512], replicated, may hold values from -0.25 to 0.25
- qkv_second: bfloat16 [512, 1536], replicated, may hold values from -1 to 1
- out_second: bfloat16 [512, 512], replicated, may hold values from -0.25 to 0.25
Outputs:
- result: bfloat16 [128, 1024, 512], P('wide', 'narrow')
Inputs may be any that keep to these rules, and one draw needn't show every extreme that they name: `counts`: the first block of every ball row has all 4 points usable. Among the blocks of one device, at most 2 have the same destination; on every device some destination receives 2 of its blocks, and some destination receives 2 blocks from every device of its narrow index.
All inputs are finite; a program needn't handle non-finite values.
Results may differ from a plain program's by a relative error of at most 0.0095.
Values may be sent and summed in bfloat16 or wider, within the bound.
A program may use at most 64 MiB of HBM per device.

v0:
```python
import math

import jax
import jax.numpy as jnp
from jax import lax
from jax.sharding import PartitionSpec as P

HEADS = 8
BLK = 4


EPSILON = 1e-06
NEGATIVE = -1e30


def rms_round(values):
    widened = values.astype(jnp.float32)
    scaled = widened * lax.rsqrt(jnp.mean(widened * widened, axis=-1, keepdims=True) + EPSILON)
    return scaled.astype(jnp.bfloat16)


def project(normed, weight):
    flat = normed.reshape(-1, normed.shape[-1])
    product = jnp.dot(flat, weight, preferred_element_type=jnp.float32)
    return product.reshape(normed.shape[:-1] + (weight.shape[1],))


def split_heads(block_rows, offset, model_width):
    head_dim = model_width // HEADS
    return block_rows[..., offset : offset + model_width].reshape(
        block_rows.shape[:-1] + (HEADS, head_dim)
    )


def usable_points(counts):
    position = lax.broadcasted_iota(jnp.int32, counts.shape + (BLK,), len(counts.shape))
    usable = position < counts[..., None]
    return usable.reshape(counts.shape[:-1] + (counts.shape[-1] * BLK,))


def pool_rows(qkv_all, counts):
    model_width = qkv_all.shape[-1] // 3
    usable = usable_points(counts)
    kv_part = qkv_all[..., model_width:].astype(jnp.float32) * usable[..., None].astype(jnp.float32)
    grouped = kv_part.reshape(counts.shape + (BLK, 2 * model_width)).sum(axis=-2)
    return (grouped / counts[..., None].astype(jnp.float32)).astype(jnp.bfloat16)


def fine_coarse(ball_qkv, fine_usable, coarse_kv):
    model_width = coarse_kv.shape[-1] // 2
    scaling = 1.0 / math.sqrt(model_width // HEADS)
    queries = split_heads(ball_qkv, 0, model_width)
    key_fine = split_heads(ball_qkv, model_width, model_width)
    value_fine = split_heads(ball_qkv, 2 * model_width, model_width)
    key_coarse = split_heads(coarse_kv, 0, model_width)
    value_coarse = split_heads(coarse_kv, model_width, model_width)
    score_fine = (
        jnp.einsum("qhe,khe->hqk", queries, key_fine, preferred_element_type=jnp.float32) * scaling
    )
    score_fine = jnp.where(fine_usable[None, None, :], score_fine, NEGATIVE)
    score_coarse = (
        jnp.einsum("qhe,khe->hqk", queries, key_coarse, preferred_element_type=jnp.float32)
        * scaling
    )
    highest = jnp.maximum(jnp.max(score_fine, axis=-1), jnp.max(score_coarse, axis=-1))[..., None]
    exp_fine = jnp.exp(score_fine - highest)
    exp_coarse = jnp.exp(score_coarse - highest)
    denominator = jnp.sum(exp_fine, axis=-1, keepdims=True) + jnp.sum(
        exp_coarse, axis=-1, keepdims=True
    )
    weight_fine = (exp_fine / denominator).astype(jnp.bfloat16)
    weight_coarse = (exp_coarse / denominator).astype(jnp.bfloat16)
    mixture = jnp.einsum(
        "hqk,khe->qhe", weight_fine, value_fine, preferred_element_type=jnp.float32
    )
    mixture = mixture + jnp.einsum(
        "hqk,khe->qhe", weight_coarse, value_coarse, preferred_element_type=jnp.float32
    )
    return mixture.reshape(mixture.shape[0], model_width).astype(jnp.bfloat16)


def ball_attention(recv_rows, row_ball, row_usable):
    total_rows = recv_rows.shape[0]
    model_width = recv_rows.shape[1] // 3
    scaling = 1.0 / math.sqrt(model_width // HEADS)
    queries = split_heads(recv_rows, 0, model_width)
    key_rows = split_heads(recv_rows, model_width, model_width)
    value_rows = split_heads(recv_rows, 2 * model_width, model_width)
    block_len = min(256, total_rows)

    def one_block(block_idx):
        offset = block_idx * block_len
        query_block = lax.dynamic_slice_in_dim(queries, offset, block_len, 0)
        ball_block = lax.dynamic_slice_in_dim(row_ball, offset, block_len, 0)
        scores = (
            jnp.einsum("qhe,khe->hqk", query_block, key_rows, preferred_element_type=jnp.float32)
            * scaling
        )
        allowed = (ball_block[:, None] == row_ball[None, :]) & row_usable[None, :]
        scores = jnp.where(allowed[None], scores, NEGATIVE)
        highest = jnp.max(scores, axis=-1, keepdims=True)
        exponent = jnp.exp(scores - highest)
        weights = (exponent / jnp.sum(exponent, axis=-1, keepdims=True)).astype(jnp.bfloat16)
        mixture = jnp.einsum(
            "hqk,khe->qhe", weights, value_rows, preferred_element_type=jnp.float32
        )
        return mixture.reshape(block_len, model_width).astype(jnp.bfloat16)

    blocks_out = lax.map(one_block, jnp.arange(total_rows // block_len, dtype=jnp.int32))
    return blocks_out.reshape(total_rows, model_width)


def on_device(
    points, counts, destination, rotated_ball, qkv_first, out_first, qkv_second, out_second
):
    model_width = points.shape[-1]
    normed_one = rms_round(points)
    qkv_one = project(normed_one, qkv_first).astype(jnp.bfloat16)
    pooled = pool_rows(qkv_one, counts)
    usable = usable_points(counts)
    pooled_all = lax.all_gather(pooled, "narrow", axis=1, tiled=True)
    attended_one = jax.vmap(fine_coarse)(qkv_one, usable, pooled_all)
    layer_one = (points.astype(jnp.float32) + project(attended_one, out_first)).astype(jnp.bfloat16)
    normed_two = rms_round(layer_one)
    wide_count = lax.axis_size("wide")
    block_count = destination.size
    capacity = max(2, 2 * block_count // wide_count)
    dest_flat = destination.reshape(block_count)
    ball_flat = rotated_ball.reshape(block_count)
    fill_flat = counts.reshape(block_count)
    onehot = (dest_flat[:, None] == jnp.arange(wide_count, dtype=jnp.int32)[None, :]).astype(
        jnp.int32
    )
    earlier = jnp.cumsum(onehot, axis=0, dtype=jnp.int32) - onehot
    rank_in = jnp.sum(earlier * onehot, axis=1, dtype=jnp.int32)
    slot_of = dest_flat * capacity + rank_in

    def packed(block_data, filler):
        buffer = jnp.full((wide_count * capacity,) + block_data.shape[1:], filler, block_data.dtype)
        return (
            buffer.at[slot_of]
            .set(block_data)
            .reshape((wide_count, capacity) + block_data.shape[1:])
        )

    ball_packed = packed(ball_flat, -1)
    fill_packed = packed(fill_flat, 0)
    qkv_two = project(normed_two, qkv_second).astype(jnp.bfloat16)
    qkv_blocks = qkv_two.reshape(block_count, BLK, 3 * model_width)
    arrived, ball_in, fill_in = (
        lax.all_to_all(packed(qkv_blocks, 0), "wide", split_axis=0, concat_axis=0, tiled=True),
        lax.all_to_all(ball_packed, "wide", split_axis=0, concat_axis=0, tiled=True),
        lax.all_to_all(fill_packed, "wide", split_axis=0, concat_axis=0, tiled=True),
    )
    recv_rows = arrived.reshape(-1, 3 * model_width)
    row_ball = jnp.broadcast_to(ball_in[..., None], ball_in.shape + (BLK,)).reshape(-1)
    row_usable = usable_points(fill_in).reshape(-1)
    mixture = ball_attention(recv_rows, row_ball, row_usable)
    returned = lax.all_to_all(
        mixture.reshape(wide_count, capacity, BLK, model_width),
        "wide",
        split_axis=0,
        concat_axis=0,
        tiled=True,
    )
    attended_two = returned.reshape(wide_count * capacity, BLK, model_width)[slot_of].reshape(
        points.shape
    )
    return (layer_one.astype(jnp.float32) + project(attended_two, out_second)).astype(jnp.bfloat16)


def solution(mesh):
    in_specs = (
        P("wide", "narrow", None),
        P("wide", "narrow"),
        P("wide", "narrow"),
        P("wide", "narrow"),
        P(),
        P(),
        P(),
        P(),
    )
    out_specs = P("wide", "narrow", None)
    return jax.shard_map(
        on_device, mesh=mesh, in_specs=in_specs, out_specs=out_specs, check_vma=False
    )
```

profile of v0, /device:TPU:1, one launch (start us, length us, event | category | flops | bytes accessed | tf_op | source)
XLA Modules:
  0.0 210.0 jit_solution(17064649044195788203)
XLA Ops:
  6.5 1.2 fusion.35
  7.8 0.7 convert_element_type.88
  8.4 0.7 lt.53
  9.4 1.6 convolution_convert_fusion.1
  11.0 1.1 convert_multiply_fusion
  12.1 1.6 reshape.243
  13.7 1.4 reduce_sum.66
  15.1 1.0 divide_convert_fusion.8
  16.1 0.8 copy.51
  17.5 0.8 scatter_custom_fusion
  18.3 0.7 all_to_all.18
  19.1 11.6 %all-to-all-start = ((s32[64,1,2]{2,1,0:T(1,128)}), s32[64,1,2]{2,1,0:T(1,128)S(1)}, u32[]{:S(2)}, u32[]{:S(2)}) async-start(s32[64,1,2]{2,1,0:T(1,128)} %bitcast.11), calls=%async_computation | async-start | bytes 65536 | tf_op jit(solution)/shard_map/all_to_all | solution.py:152
  31.1 0.8 copy.48
  32.3 27.9 %all-gather.2.cloned.1.call-done = bf16[2,256,1024]{2,0,1:T(2,128)(2,1)} async-done(((bf16[2,32,1024]{2,0,1:T(2,128)(2,1)}), bf16[2,256,1024]{2,0,1:T(2,128)(2,1)}) %all-gather.2.cloned.1.call-update) | async-done | bytes 1048592 | tf_op jit(solution)/shard_map/all_gather | solution.py:121
  60.2 2.7 %fusion.57 = (bf16[2,256,512]{2,0,1:T(2,128)(2,1)S(1)}, bf16[2,256,512]{2,0,1:T(2,128)(2,1)}) fusion(bf16[2,256,1024]{2,0,1:T(2,128)(2,1)} %all-gather.2.cloned.1.call-done), kind=kLoop, calls=%fused_computation.79 | loop fusion | bytes 2097152 | tf_op jit(solution)/shard_map/vmap()/slice | solution.py:30
  63.0 2.0 copy.52
  65.0 1.6 multiply_reduce_fusion
  66.8 1.2 copy-done.1
  67.9 0.7 fusion.26
  68.7 1.2 copy.54
  70.2 1.3 copy-done.2
  71.6 1.1 fusion.30
  73.1 0.8 copy-done.3
  74.1 0.6 convolution_convert_fusion
  74.9 1.6 broadcast_in_dim.71
  76.4 8.1 %scatter_fusion = bf16[128,4,1536]{2,1,0:T(4,128)(2,1)} fusion(bf16[128,4,1536]{2,1,0:T(4,128)(2,1)} %broadcast_in_dim.71, s32[64]{0:T(128)S(1)} %fusion.44, bf16[64,4,1536]{2,1,0:T(4,128)(2,1)S(1)} %reshape.284), kind=kCustom, calls=%fused_computation.3 | custom fusion | bytes 2359552 | tf_op jit(solution)/shard_map/scatter | solution.py:142
  84.5 15.0 %all-to-all-start.2 = ((bf16[64,2,4,1536]{3,2,1,0:T(4,128)(2,1)}), bf16[64,2,4,1536]{3,2,1,0:T(4,128)(2,1)S(1)}, u32[]{:S(2)}, u32[]{:S(2)}) async-start(bf16[64,2,4,1536]{3,2,1,0:T(4,128)(2,1)} %bitcast.14), calls=%async_computation.2 | async-start | bytes 3145728 | tf_op jit(solution)/shard_map/all_to_all | solution.py:151
  99.7 0.8 scatter_custom_fusion.1
  100.4 0.8 all_to_all.20
  101.6 37.7 %all-to-all-done.2 = bf16[64,2,4,1536]{3,2,1,0:T(4,128)(2,1)S(1)} async-done(((bf16[64,2,4,1536]{3,2,1,0:T(4,128)(2,1)}), bf16[64,2,4,1536]{3,2,1,0:T(4,128)(2,1)S(1)}, u32[]{:S(2)}, u32[]{:S(2)}) %all-to-all-start.2) | async-done | bytes 1572896 | tf_op jit(solution)/shard_map/all_to_all | solution.py:151
  139.4 6.1 %all-to-all-start.1 = ((s32[64,1,2]{2,1,0:T(1,128)}), s32[64,1,2]{2,1,0:T(1,128)S(1)}, u32[]{:S(2)}, u32[]{:S(2)}) async-start(s32[64,1,2]{2,1,0:T(1,128)} %bitcast.18), calls=%async_computation.1 | async-start | bytes 65536 | tf_op jit(solution)/shard_map/all_to_all | solution.py:153
  145.5 1.4 reshape.251
  146.8 1.5 fusion.56
  148.3 1.0 copy.59
  149.3 1.0 copy.60
  150.6 4.1 %all-to-all-done.1 = s32[64,1,2]{2,1,0:T(1,128)S(1)} async-done(((s32[64,1,2]{2,1,0:T(1,128)}), s32[64,1,2]{2,1,0:T(1,128)S(1)}, u32[]{:S(2)}, u32[]{:S(2)}) %all-to-all-start.1) | async-done | bytes 544 | tf_op jit(solution)/shard_map/all_to_all | solution.py:153
  154.7 20.9 %while.11 = (s32[]{:T(128)}, bf16[2,256,512]{2,1,0:T(8,128)(2,1)}, s32[2]{0:T(128)S(1)}, s32[512]{0:T(512)S(1)}, bf16[512,8,64]{0,2,1:T(8,128)(2,1)S(1)}, /*inde...) while((s32[]{:T(128)}, bf16[2,256,512]{2,1,0:T(8,128)(2,1)}, ...), condition=%wide.region_15.16_spmd.clone, body=%wide.region_12.15_spmd.clone.sunk | while | flops 275121152 | bytes 11303615 | solution.py:109
  156.7 4.5 %fusion.79 = (f32[8,256]{1,0:T(8,128)S(1)}, f32[8,256,512]{2,1,0:T(8,128)}) fusion(pred[256,512]{1,0:T(8,128)(4,1)S(1)} %compare_and_fusion.2, bf16[512,8,64]{0,2,1:T(8,128)(2,1)} %get-tuple-element.229, bf16[512,8,64]{0,2,1:T(8,128)(2,1)S(1)} %get-tuple-element.228, s32[]{:T(128)S(6)} %select_n.46), kind=kOutput, calls=%fused_computation.77.clone.1 | convolution fusion | flops 138412544 | bytes 5120004 | tf_op jit(solution)/shard_map/while/body/eval_jaxpr/sub | solution.py:102
  161.2 3.0 %fusion.80 = bf16[8,256,64]{1,2,0:T(8,128)(2,1)S(1)} fusion(bf16[512,8,64]{0,2,1:T(8,128)(2,1)S(1)} %get-tuple-element.230, f32[8,256,512]{2,1,0:T(8,128)} %get-tuple-element.196, f32[8,256]{1,0:T(8,128)S(1)} %get-tuple-element.197), kind=kOutput, calls=%fused_computation.15.clone.1 | convolution fusion | flops 136445952 | bytes 4988928 | tf_op jit(solution)/shard_map/while/body/eval_jaxpr/hqk,khe->qhe/dot_general | solution.py:104
  164.4 0.7 constant_dynamic-update-slice_fusion.2
  167.2 4.5 %fusion.79 = (f32[8,256]{1,0:T(8,128)S(1)}, f32[8,256,512]{2,1,0:T(8,128)}) fusion(pred[256,512]{1,0:T(8,128)(4,1)S(1)} %compare_and_fusion.2, bf16[512,8,64]{0,2,1:T(8,128)(2,1)} %get-tuple-element.229, bf16[512,8,64]{0,2,1:T(8,128)(2,1)S(1)} %get-tuple-element.228, s32[]{:T(128)S(6)} %select_n.46), kind=kOutput, calls=%fused_computation.77.clone.1 | convolution fusion | flops 138412544 | bytes 5120004 | tf_op jit(solution)/shard_map/while/body/eval_jaxpr/sub | solution.py:102
  171.7 3.0 %fusion.80 = bf16[8,256,64]{1,2,0:T(8,128)(2,1)S(1)} fusion(bf16[512,8,64]{0,2,1:T(8,128)(2,1)S(1)} %get-tuple-element.230, f32[8,256,512]{2,1,0:T(8,128)} %get-tuple-element.196, f32[8,256]{1,0:T(8,128)S(1)} %get-tuple-element.197), kind=kOutput, calls=%fused_computation.15.clone.1 | convolution fusion | flops 136445952 | bytes 4988928 | tf_op jit(solution)/shard_map/while/body/eval_jaxpr/hqk,khe->qhe/dot_general | solution.py:104
  174.9 0.7 constant_dynamic-update-slice_fusion.2
  175.6 2.1 reshape_reshape.4
  177.7 6.2 %all-to-all-start.3 = ((bf16[64,2,4,512]{3,2,1,0:T(4,128)(2,1)}), bf16[64,2,4,512]{3,2,1,0:T(4,128)(2,1)S(1)}, u32[]{:S(2)}, u32[]{:S(2)}) async-start(bf16[64,2,4,512]{3,2,1,0:T(4,128)(2,1)} %reshape_reshape.4), calls=%async_computation.3 | async-start | bytes 1048576 | tf_op jit(solution)/shard_map/all_to_all | solution.py:159
  183.9 17.3 %all-to-all-done.3 = bf16[64,2,4,512]{3,2,1,0:T(4,128)(2,1)S(1)} async-done(((bf16[64,2,4,512]{3,2,1,0:T(4,128)(2,1)}), bf16[64,2,4,512]{3,2,1,0:T(4,128)(2,1)S(1)}, u32[]{:S(2)}, u32[]{:S(2)}) %all-to-all-start.3) | async-done | bytes 524320 | tf_op jit(solution)/shard_map/all_to_all | solution.py:159
  201.3 0.8 gather_fusion
  202.1 1.0 fusion.33
  (80 shorter events, 6.8 us)
Async XLA Ops:
  6.5 2.9 %copy-start = (bf16[512,1536]{1,0:T(8,128)(2,1)S(1)}, bf16[512,1536]{1,0:T(8,128)(2,1)}, u32[]{:S(2)}) copy-start(bf16[512,1536]{1,0:T(8,128)(2,1)} %param.14) | copy-start | bytes 4718596
  6.5 53.7 %all-gather.2.cloned.1.call-start = ((), (), s32[]{:S(2)}) async-start(), calls=%async_computation.4 | async-start | bytes 1179648 | tf_op jit(solution)/shard_map/all_gather | solution.py:121
  12.1 4.8 %copy-start.13 = (s32[2,32]{1,0:T(2,128)S(1)}, s32[2,32]{1,0:T(2,128)}, u32[]{:S(2)}) copy-start(s32[2,32]{1,0:T(2,128)} %param.12) | copy-start | bytes 772
  12.1 5.0 %copy-start.14 = (s32[2,32]{1,0:T(2,128)S(1)}, s32[2,32]{1,0:T(2,128)}, u32[]{:S(2)}) copy-start(s32[2,32]{1,0:T(2,128)} %param.13) | copy-start | bytes 772
  19.1 65.5 %all-to-all-start = ((s32[64,1,2]{2,1,0:T(1,128)}), s32[64,1,2]{2,1,0:T(1,128)S(1)}, u32[]{:S(2)}, u32[]{:S(2)}) async-start(s32[64,1,2]{2,1,0:T(1,128)} %bitcast.11), calls=%async_computation | async-start | bytes 65536 | tf_op jit(solution)/shard_map/all_to_all | solution.py:152
  66.6 1.4 copy-start.1
  66.6 3.3 %copy-start.11 = (bf16[2,128,512]{1,2,0:T(8,128)(2,1)S(1)}, bf16[2,128,512]{1,2,0:T(8,128)(2,1)}, u32[]{:S(2)}) copy-start(bf16[2,128,512]{1,2,0:T(8,128)(2,1)} %copy.48) | copy-start | bytes 786436
  69.9 1.6 copy-start.2
  69.9 1.7 copy-start.9
  71.6 1.1 copy-start.5
  71.6 1.1 copy-start.10
  72.7 1.4 copy-start.6
  73.1 0.8 copy-start.3
  84.5 15.1 %copy-start.12 = (s32[2,32]{1,0:T(2,128)S(1)}, s32[2,32]{1,0:T(2,128)}, u32[]{:S(2)}) copy-start(s32[2,32]{1,0:T(2,128)} %param.11) | copy-start | bytes 772
  84.5 54.8 %all-to-all-start.2 = ((bf16[64,2,4,1536]{3,2,1,0:T(4,128)(2,1)}), bf16[64,2,4,1536]{3,2,1,0:T(4,128)(2,1)S(1)}, u32[]{:S(2)}, u32[]{:S(2)}) async-start(bf16[64,2,4,1536]{3,2,1,0:T(4,128)(2,1)} %bitcast.14), calls=%async_computation.2 | async-start | bytes 3145728 | tf_op jit(solution)/shard_map/all_to_all | solution.py:151
  139.4 15.3 %all-to-all-start.1 = ((s32[64,1,2]{2,1,0:T(1,128)}), s32[64,1,2]{2,1,0:T(1,128)S(1)}, u32[]{:S(2)}, u32[]{:S(2)}) async-start(s32[64,1,2]{2,1,0:T(1,128)} %bitcast.18), calls=%async_computation.1 | async-start | bytes 65536 | tf_op jit(solution)/shard_map/all_to_all | solution.py:153
  149.3 5.4 %copy-start.8 = (bf16[512,512]{0,1:T(8,128)(2,1)S(1)}, bf16[512,512]{0,1:T(8,128)(2,1)}, u32[]{:S(2)}) copy-start(bf16[512,512]{0,1:T(8,128)(2,1)} %copy.59) | copy-start | bytes 1572868
  175.6 26.5 %copy-start.4 = (f32[2,128,512]{2,1,0:T(8,128)S(1)}, f32[2,128,512]{2,1,0:T(8,128)}, u32[]{:S(2)}) copy-start(f32[2,128,512]{2,1,0:T(8,128)} %copy-done.3) | copy-start | bytes 1572868
  175.6 26.5 %copy-start.7 = (bf16[512,512]{1,0:T(8,128)(2,1)S(1)}, bf16[512,512]{1,0:T(8,128)(2,1)}, u32[]{:S(2)}) copy-start(bf16[512,512]{1,0:T(8,128)(2,1)} %param.17) | copy-start | bytes 1572868
  177.7 23.6 %all-to-all-start.3 = ((bf16[64,2,4,512]{3,2,1,0:T(4,128)(2,1)}), bf16[64,2,4,512]{3,2,1,0:T(4,128)(2,1)S(1)}, u32[]{:S(2)}, u32[]{:S(2)}) async-start(bf16[64,2,4,512]{3,2,1,0:T(4,128)(2,1)} %reshape_reshape.4), calls=%async_computation.3 | async-start | bytes 1048576 | tf_op jit(solution)/shard_map/all_to_all | solution.py:159
Sparse Core Ops, SparseCore 0:
  17.0 43.1 all-gather.1
where the time goes:
time: 211 us; the launch traced here: 210 us
  waiting for transfers between devices  87.1 us (41%)
  local copies, waits for them, and re-layouts  39.5 us (19%)
  starting transfers between devices  39 us (18%)
  matrix products  22 us (10%)
  between operations  13.7 us (6%)
  other arithmetic  7.28 us (3%)
    all_to_all x1, waiting for transfers between devices, on_device(): lax.all_to_all(packed(qkv_blocks, 0), 'wide', split_axis=0, concat_axis=0...  37.7 us
    all_gather x1, waiting for transfers between devices, on_device(): pooled_all = lax.all_gather(pooled, 'narrow', axis=1, tiled=True)  27.9 us
    all_to_all x1, waiting for transfers between devices, on_device(): lax.all_to_all(mixture.reshape(wide_count, capacity, BLK, model_width), '...  17.3 us
    all_to_all x1, starting transfers between devices, on_device(): lax.all_to_all(packed(qkv_blocks, 0), 'wide', split_axis=0, concat_axis=0...  15 us
    all_to_all x1, starting transfers between devices, on_device(): lax.all_to_all(ball_packed, 'wide', split_axis=0, concat_axis=0, tiled=True)  11.6 us
    slice x11, local copies, waits for them, and re-layouts, split_heads(): block_rows[..., offset:offset + model_width]  10.9 us
    scatter x3, local copies, waits for them, and re-layouts, packed(): return buffer.at[slot_of].set(block_data).reshape((wide_count, capacity)...  9.61 us
    sub x2, matrix products, one_block(): exponent = jnp.exp(scores - highest)  9.07 us
  transfers between devices with their start and end apart: 5, of which 4 were waited for; matrix products, arithmetic and copies ran while one was open for 14% of the time, Pallas kernels for 0%

commit v1 on v0

v1 whole, which is shorter than its diff:
```python
import functools
import math

import jax
import jax.numpy as jnp
from jax import lax
from jax.experimental import pallas as pl
from jax.experimental.pallas import tpu as pltpu
from jax.sharding import PartitionSpec as P

HEADS = 8
BLK = 4
NX, NY, NZ = 4, 8, 8
WIDE = 2 * NX * NY
ROWS = 256
BLOCKS = 64
SHARE = 128
WIDTH = 512
SLOT = 2 * BLK
SLOTROWS = WIDE * SLOT
PAIRS = HEADS // 2
DY = (0, 4, 1, 7, 2, 6, 3, 5)
GROUPS = 4
GSLOTS = WIDE // GROUPS
GROWS = GSLOTS * SLOT

EPSILON = 1e-06
NEGATIVE = -1e30
MESH = pl.DeviceIdType.MESH
F32 = jnp.float32
BF16 = jnp.bfloat16


def iota(shape, axis):
    return lax.broadcasted_iota(jnp.int32, shape, axis)


def rms_round(values):
    scaled = values * lax.rsqrt(jnp.mean(values * values, axis=-1, keepdims=True) + EPSILON)
    return scaled.astype(BF16)


def dot(left, right):
    return jnp.dot(left, right, preferred_element_type=F32)


def dot_t(left, right):
    return lax.dot_general(left, right, (((1,), (1,)), ((), ())), preferred_element_type=F32)


def column(ref, rows, per):
    values = ref[...].astype(F32)
    half = values.shape[1]
    block = iota((rows, half), 0) // per
    lane = iota((rows, half), 1)
    first = jnp.where(block == lane, values[0:1, :], 0.0)
    second = jnp.where(block == lane + half, values[1:2, :], 0.0)
    return jnp.sum(first + second, axis=1, keepdims=True)


def to_lanes(col):
    rows = col.shape[0]
    eye = iota((rows, rows), 0) == iota((rows, rows), 1)
    return jnp.sum(jnp.where(eye, col, 0.0), axis=0, keepdims=True)


def two_heads(pair):
    low = iota(pair.shape, 1) < 64
    zero = jnp.zeros_like(pair)
    return jnp.concatenate([jnp.where(low, pair, zero), jnp.where(low, zero, pair)], axis=0)


def softmax_values(scores, values):
    highest = jnp.max(scores, axis=1, keepdims=True)
    weights = jnp.exp(scores - highest).astype(BF16)
    ones = jnp.ones((values.shape[0], 128), BF16)
    mixed = dot(weights, jnp.concatenate([values, ones], axis=1))
    mixed = mixed[:, :128] / mixed[:, 128:]
    half = mixed.shape[0] // 2
    low = iota((half, 128), 1) < 64
    return jnp.where(low, mixed[:half], mixed[half:])


def kernel(
    pts_h, cnt_h, dst_h, rot_h, w1_h, o1_h, w2_h, o2_h,
    out_ref,
    pts, cnt, dst, rot, w1, o1, w2, o2,
    ag, meta_s, meta_r, snd, rcv, bsnd, brcv, qkv1, qkv2, unpack,
    load_sem, ring_send, ring_recv, meta_send, meta_recv, fwd_send, fwd_recv, back_send, back_recv,
):
    wide = lax.axis_index("wide")
    z = lax.axis_index("narrow")
    x_me = wide // (2 * NY)
    y_me = (wide // 2) % NY
    c_me = wide % 2

    loads = [
        pltpu.make_async_copy(src, dest, load_sem.at[i])
        for i, (src, dest) in enumerate(
            ((cnt_h, cnt), (dst_h, dst), (rot_h, rot), (pts_h, pts), (w1_h, w1), (o1_h, o1), (w2_h, w2), (o2_h, o2))
        )
    ]
    for load in loads:
        load.start()

    def peer(dy, i):
        return ((x_me + i // 2) % NX) * (2 * NY) + ((y_me + dy) % NY) * 2 + (c_me + i) % 2

    def source(dy, i):
        return ((x_me + NX - i // 2) % NX) * (2 * NY) + ((y_me + NY - dy) % NY) * 2 + (c_me + i) % 2

    def each_slot(visit, groups=range(GROUPS)):
        for g in groups:
            for h in range(2):
                j = 2 * g + h

                def one(i, carry, j=j, g=g):
                    visit(8 * j + i, g, DY[j], i)
                    return carry

                lax.fori_loop(1 if j == 0 else 0, 8, one, 0)

    barrier = pltpu.get_barrier_semaphore()
    up, down = (z + 1) % NZ, (z + NZ - 1) % NZ
    for other in (up, down):
        pl.semaphore_signal(barrier, inc=1, device_id=(wide, other), device_id_type=MESH)

    def greet(k, g, dy, i):
        pl.semaphore_signal(barrier, inc=1, device_id=(peer(dy, i), z), device_id_type=MESH)

    each_slot(greet)

    loads[0].wait()
    cnt64 = column(cnt, BLOCKS, 1)
    r_b, r_l = iota((BLOCKS, ROWS), 0), iota((BLOCKS, ROWS), 1)
    pool = (r_l // BLK == r_b) & ((r_l % BLK).astype(F32) < cnt64)
    pool = jnp.where(pool, 1.0, 0.0).astype(BF16)
    loads[3].wait()
    normed_one = rms_round(pts[...].astype(F32))
    pooled = (dot(pool, normed_one) / cnt64).astype(BF16)
    ag[0] = pooled.reshape(2, BLOCKS // 2, WIDTH)

    pl.semaphore_wait(barrier, WIDE - 1 + 2)

    def hop(way, step, ball):
        here = (step if way == 0 else (NZ - step) % NZ)
        there = step + 1 if way == 0 else NZ - 1 - step
        return pltpu.make_async_remote_copy(
            src_ref=ag.at[here, ball],
            dst_ref=ag.at[there, ball],
            send_sem=ring_send.at[way, step, ball],
            recv_sem=ring_recv.at[there, ball],
            device_id=(wide, up if way == 0 else down),
            device_id_type=MESH,
        )

    sent = []

    def ring(step):
        for ball in range(2):
            for way in range(2):
                if step == 3 and ball != way:
                    continue
                if step > 0:
                    hop(way, step - 1, ball).wait_recv()
                copy = hop(way, step, ball)
                copy.start()
                sent.append(copy)

    ring(0)

    loads[1].wait()
    loads[2].wait()
    cnt_col = column(cnt, ROWS, BLK)
    rot_col = column(rot, ROWS, BLK)
    dst_col = column(dst, ROWS, BLK)
    q_r, q_l = iota((ROWS, ROWS), 0), iota((ROWS, ROWS), 1)
    same = (dst_col == to_lanes(dst_col)) & (q_l // BLK < q_r // BLK)
    rank = jnp.sum(jnp.where(same, 1.0 / BLK, 0.0), axis=1, keepdims=True)
    dst_i = dst_col.astype(jnp.int32)
    d_x = ((dst_i // (2 * NY)) + NX - x_me) % NX
    d_y = ((dst_i // 2) % NY + NY - y_me) % NY
    d_c = (dst_i + c_me) % 2
    turn = jnp.where(d_y < 4, 2 * d_y, (17 - 2 * d_y) % 8)
    slot = (8 * turn + 2 * d_x + d_c) * SLOT + iota((ROWS, 1), 0) % BLK
    slot_col = slot.astype(F32) + rank * BLK
    slot_lane = to_lanes(slot_col)
    unpack[...] = jnp.where(iota((ROWS, SLOTROWS), 1).astype(F32) == slot_col, 1.0, 0.0).astype(BF16)
    pack = jnp.where(iota((SLOTROWS, ROWS), 0).astype(F32) == slot_lane, 1.0, 0.0).astype(BF16)

    ring(1)

    in_first = jnp.where(rot_col == 0.0, 1.0, 0.0)
    usable = jnp.where((iota((ROWS, 1), 0) % BLK).astype(F32) < cnt_col, 1.0, 0.0)
    lane = iota((ROWS, 128), 1)
    meta = jnp.where(lane == 0, in_first, 0.0)
    meta = jnp.where(lane == 1, 1.0 - in_first, meta)
    meta = jnp.where(lane == 2, in_first * usable, meta)
    meta = jnp.where(lane == 3, (1.0 - in_first) * usable, meta)
    meta_slots = dot(pack, meta.astype(BF16)).reshape(WIDE, SLOT, 128).astype(BF16)
    meta_s[...] = meta_slots
    meta_r[0] = meta_slots[0]

    def move(src, dest, k, send_sem, recv_sem, to):
        return pltpu.make_async_remote_copy(
            src_ref=src.at[k],
            dst_ref=dest.at[k],
            send_sem=send_sem,
            recv_sem=recv_sem,
            device_id=(to, z),
            device_id_type=MESH,
        )

    def send_meta(k, g, dy, i):
        move(meta_s, meta_r, k, meta_send, meta_recv, peer(dy, i)).start()

    each_slot(send_meta)

    loads[4].wait()
    qkv1[...] = dot(normed_one, w1[...]).astype(BF16)
    ring(2)
    bias = jnp.where(to_lanes(usable) > 0.0, 0.0, NEGATIVE)
    ring(3)
    for ball in range(2):
        hop(0, 2, 1 - ball).wait_recv() if ball == 0 else hop(1, 2, 1 - ball).wait_recv()
    hop(0, 3, 0).wait_recv()
    hop(1, 3, 1).wait_recv()

    attended = []
    for ball in range(2):
        pooled_all = ag[:, ball].reshape(NZ * BLOCKS // 2, WIDTH)
        pooled_kv = dot(pooled_all, w1[:, WIDTH:]).astype(BF16)
        mine = pl.ds(ball * SHARE, SHARE)
        bias_ball = jnp.concatenate(
            [bias[:, ball * SHARE : (ball + 1) * SHARE], jnp.zeros((1, NZ * BLOCKS // 2), F32)], axis=1
        )
        parts = []
        for pair in range(PAIRS):
            at = pair * 128
            query = two_heads(qkv1[mine, at : at + 128] * 0.125)
            key = jnp.concatenate(
                [qkv1[mine, WIDTH + at : WIDTH + at + 128], pooled_kv[:, at : at + 128]], axis=0
            )
            value = jnp.concatenate(
                [
                    qkv1[mine, 2 * WIDTH + at : 2 * WIDTH + at + 128],
                    pooled_kv[:, WIDTH + at : WIDTH + at + 128],
                ],
                axis=0,
            )
            parts.append(softmax_values(dot_t(query, key) + bias_ball, value).astype(BF16))
        attended.append(jnp.concatenate(parts, axis=1))
    attended_one = jnp.concatenate(attended, axis=0)
    loads[5].wait()
    layer_one = (pts[...].astype(F32) + dot(attended_one, o1[...])).astype(BF16)
    pts[...] = layer_one
    normed_two = rms_round(layer_one.astype(F32))
    slots = dot(pack, normed_two).reshape(WIDE, SLOT, WIDTH).astype(BF16)
    snd[...] = slots
    rcv[0] = slots[0]

    def send_rows(k, g, dy, i):
        move(snd, rcv, k, fwd_send, fwd_recv.at[g], peer(dy, i)).start()

    each_slot(send_rows)

    def arrived(src, dest, first, count, send_sem, recv_sem):
        return pltpu.make_async_remote_copy(
            src_ref=src.at[pl.ds(first, count)],
            dst_ref=dest.at[pl.ds(first, count)],
            send_sem=send_sem,
            recv_sem=recv_sem,
            device_id=(peer(0, 1), z),
            device_id_type=MESH,
        )

    def group(g):
        return (1, GSLOTS - 1) if g == 0 else (g * GSLOTS, GSLOTS)

    arrived(meta_s, meta_r, 1, WIDE - 1, meta_send, meta_recv).wait_recv()
    marks = meta_r[...].astype(F32).reshape(SLOTROWS, 128)
    lanes = iota((SLOTROWS, 128), 1)
    use = (lanes == 2) | (lanes == 3)
    query_mark = jnp.where(use, pltpu.roll(marks, 2, 1), 0.0).astype(BF16)
    key_mark = jnp.where(use, (1.0 - marks) * NEGATIVE, 0.0).astype(BF16)

    loads[6].wait()
    for g in range(GROUPS):
        first, count = group(g)
        arrived(snd, rcv, first, count, fwd_send, fwd_recv.at[g]).wait_recv()
        rows = rcv[g * GSLOTS : (g + 1) * GSLOTS].astype(F32).reshape(GROWS, WIDTH).astype(BF16)
        qkv2[g * GROWS : (g + 1) * GROWS, :] = dot(rows, w2[...]).astype(BF16)

    for g in range(GROUPS):
        mine = slice(g * GROWS, (g + 1) * GROWS)
        mark = query_mark[mine]
        parts = []
        for pair in range(PAIRS):
            at = pair * 128
            query = two_heads(qkv2[mine, at : at + 128] * 0.125)
            query = jnp.concatenate([query, jnp.concatenate([mark, mark], axis=0)], axis=1)
            key = jnp.concatenate([qkv2[:, WIDTH + at : WIDTH + at + 128], key_mark], axis=1)
            value = qkv2[:, 2 * WIDTH + at : 2 * WIDTH + at + 128]
            parts.append(softmax_values(dot_t(query, key), value))
        mixture = jnp.concatenate(parts, axis=1).reshape(GSLOTS, SLOT, WIDTH).astype(BF16)
        bsnd[g * GSLOTS : (g + 1) * GSLOTS] = mixture
        if g == 0:
            brcv[0] = mixture[0]

        def send_back(k, g, dy, i):
            move(bsnd, brcv, k, back_send, back_recv.at[g], source(dy, i)).start()

        each_slot(send_back, (g,))

    loads[7].wait()
    total = jnp.zeros((ROWS, WIDTH), F32)
    for g in range(GROUPS):
        first, count = group(g)
        arrived(bsnd, brcv, first, count, back_send, back_recv.at[g]).wait_recv()
        rows = brcv[g * GSLOTS : (g + 1) * GSLOTS].astype(F32).reshape(GROWS, WIDTH).astype(BF16)
        total = total + dot(unpack[:, g * GROWS : (g + 1) * GROWS], rows)
    out_ref[...] = (pts[...].astype(F32) + dot(total.astype(BF16), o2[...])).astype(BF16)

    for copy in sent:
        copy.wait_send()
    arrived(meta_s, meta_r, 1, WIDE - 1, meta_send, meta_recv).wait_send()
    arrived(snd, rcv, 1, WIDE - 1, fwd_send, fwd_recv.at[0]).wait_send()
    arrived(bsnd, brcv, 1, WIDE - 1, back_send, back_recv.at[0]).wait_send()


def on_device(points, counts, destination, rotated_ball, qkv_first, out_first, qkv_second, out_second):
    rows = points.reshape(ROWS, WIDTH)
    dma = pltpu.SemaphoreType.DMA
    hbm = pl.BlockSpec(memory_space=pltpu.MemorySpace.HBM)
    result = pl.pallas_call(
        kernel,
        out_shape=jax.ShapeDtypeStruct((ROWS, WIDTH), BF16),
        in_specs=[hbm] * 8,
        out_specs=pl.BlockSpec(memory_space=pltpu.VMEM),
        scratch_shapes=[
            pltpu.VMEM((ROWS, WIDTH), BF16),
            pltpu.VMEM((2, 32), jnp.int32),
            pltpu.VMEM((2, 32), jnp.int32),
            pltpu.VMEM((2, 32), jnp.int32),
            pltpu.VMEM((WIDTH, 3 * WIDTH), BF16),
            pltpu.VMEM((WIDTH, WIDTH), BF16),
            pltpu.VMEM((WIDTH, 3 * WIDTH), BF16),
            pltpu.VMEM((WIDTH, WIDTH), BF16),
            pltpu.VMEM((NZ, 2, BLOCKS // 2, WIDTH), BF16),
            pltpu.VMEM((WIDE, SLOT, 128), BF16),
            pltpu.VMEM((WIDE, SLOT, 128), BF16),
            pltpu.VMEM((WIDE, SLOT, WIDTH), BF16),
            pltpu.VMEM((WIDE, SLOT, WIDTH), BF16),
            pltpu.VMEM((WIDE, SLOT, WIDTH), BF16),
            pltpu.VMEM((WIDE, SLOT, WIDTH), BF16),
            pltpu.VMEM((ROWS, 3 * WIDTH), BF16),
            pltpu.VMEM((SLOTROWS, 3 * WIDTH), BF16),
            pltpu.VMEM((ROWS, SLOTROWS), BF16),
            dma((8,)),
            dma((2, 4, 2)),
            dma((NZ, 2)),
            dma,
            dma,
            dma,
            dma((GROUPS,)),
            dma,
            dma((GROUPS,)),
        ],
        compiler_params=pltpu.CompilerParams(
            collective_id=0, has_side_effects=True, vmem_limit_bytes=48 * 1024 * 1024
        ),
    )(rows, counts, destination, rotated_ball, qkv_first, out_first, qkv_second, out_second)
    return result.reshape(points.shape)


def solution(mesh):
    in_specs = (
        P("wide", "narrow", None),
        P("wide", "narrow"),
        P("wide", "narrow"),
        P("wide", "narrow"),
        P(),
        P(),
        P(),
        P(),
    )
    out_specs = P("wide", "narrow", None)
    return jax.shard_map(
        on_device, mesh=mesh, in_specs=in_specs, out_specs=out_specs, check_vma=False
    )
```

time: 211 us -> 74 us (0.35)
  waiting for transfers between devices: 87.1 us -> 0 us
  Pallas kernels: 0 us -> 64.6 us
  starting transfers between devices: 39 us -> 0 us
  local copies, waits for them, and re-layouts: 39.5 us -> 8.59 us
  matrix products: 22 us -> 0 us
  between operations: 13.7 us -> 0.02 us
  other arithmetic: 7.28 us -> 0 us
    pallas_call x0 -> x1, Pallas kernels: none -> 64.6 us  [on_device(): pl.pallas_call(kernel, out_shape=jax.ShapeDtypeStruct((ROWS, WIDTH), BF16...]
    all_to_all x4 -> x0, waiting for transfers between devices: 59.2 us -> none  [the longest x1 37.7 us: on_device(): lax.all_to_all(packed(qkv_blocks, 0), 'wide', split_axis=0, concat_axis=0...]
    all_to_all x4 -> x0, starting transfers between devices: 39 us -> none  [the longest x1 15 us: on_device(): lax.all_to_all(packed(qkv_blocks, 0), 'wide', split_axis=0, concat_axis=0...]
    all_gather x1 -> x0, waiting for transfers between devices: 27.9 us -> none  [on_device(): pooled_all = lax.all_gather(pooled, 'narrow', axis=1, tiled=True)]
    dot_general x10 -> x0, matrix products: 13 us -> none  [the longest x2 6.05 us: one_block(): jnp.einsum('hqk,khe->qhe', weights, value_rows, preferred_element_type=jn...]
    slice x11 -> x0, local copies, waits for them, and re-layouts: 10.9 us -> none  [split_heads(): block_rows[..., offset:offset + model_width]]
    scatter x3 -> x0, local copies, waits for them, and re-layouts: 9.61 us -> none  [packed(): return buffer.at[slot_of].set(block_data).reshape((wide_count, capacity)...]
    sub x2 -> x0, matrix products: 9.07 us -> none  [one_block(): exponent = jnp.exp(scores - highest)]
  transfers between devices with their start and end apart: 5 -> 0, of which waited for: 4 -> 0; matrix products, arithmetic and copies ran while one was open for 14% -> 0% of each run, Pallas kernels for 0% -> 0%
where the time goes in v1:
time: 74 us; the launch traced here: 73.2 us
  Pallas kernels  64.6 us (87%)
  local copies, waits for them, and re-layouts  8.59 us (12%)
    pallas_call x1, Pallas kernels, on_device(): pl.pallas_call(kernel, out_shape=jax.ShapeDtypeStruct((ROWS, WIDTH), BF16...  64.6 us
    unnamed x17, local copies, waits for them, and re-layouts  8.59 us

profile of v1, /device:TPU:1, one launch (start us, length us, event | category | flops | bytes accessed | tf_op | source)
XLA Modules:
  0.0 73.2 jit_solution(5242164157430056898)
XLA Ops:
  0.0 0.0 copy-start
  0.0 1.4 %copy-done = bf16[512,1536]{1,0:T(8,128)(2,1)S(1)} copy-done((bf16[512,1536]{1,0:T(8,128)(2,1)S(1)}, bf16[512,1536]{1,0:T(8,128)(2,1)}, u32[]{:S(2)}) %copy-start) | copy-done | bytes 1572888
  1.4 0.0 copy-start.1
  1.4 1.4 %copy-done.1 = bf16[512,1536]{1,0:T(8,128)(2,1)S(1)} copy-done((bf16[512,1536]{1,0:T(8,128)(2,1)S(1)}, bf16[512,1536]{1,0:T(8,128)(2,1)}, u32[]{:S(2)}) %copy-start.1) | copy-done | bytes 1572888
  2.8 0.0 copy-start.2
  2.8 1.0 %copy-done.2 = bf16[512,512]{1,0:T(8,128)(2,1)S(1)} copy-done((bf16[512,512]{1,0:T(8,128)(2,1)S(1)}, bf16[512,512]{1,0:T(8,128)(2,1)}, u32[]{:S(2)}) %copy-start.2) | copy-done | bytes 524312
  3.9 0.0 copy-start.3
  3.9 1.0 %copy-done.3 = bf16[512,512]{1,0:T(8,128)(2,1)S(1)} copy-done((bf16[512,512]{1,0:T(8,128)(2,1)S(1)}, bf16[512,512]{1,0:T(8,128)(2,1)}, u32[]{:S(2)}) %copy-start.3) | copy-done | bytes 524312
  4.9 0.0 copy-start.4
  4.9 0.9 %copy-done.4 = bf16[2,128,512]{2,1,0:T(8,128)(2,1)S(1)} copy-done((bf16[2,128,512]{2,1,0:T(8,128)(2,1)S(1)}, bf16[2,128,512]{2,1,0:T(8,128)(2,1)}, u32[]{:S(2)}) %copy-start.4) | copy-done | bytes 262168
  5.9 0.0 copy-start.5
  5.9 0.7 copy-done.5
  6.5 0.0 copy-start.6
  6.5 0.7 copy-done.6
  7.2 0.0 copy-start.7
  7.2 0.7 copy-done.7
  7.9 64.6 %shard_map.82 = bf16[256,512]{1,0:T(8,128)(2,1)S(1)} custom-call(bf16[256,512]{1,0:T(8,128)(2,1)S(1)} %bitcast.3, s32[2,32]{1,0:T(2,128)S(1)} %copy-done.5, s32[2,32]{1,0:T(2,128)S(1)} %copy-done.6, s32[2,32]{1,0:T(2,128)S(1)} %copy-done.7, bf16[512,1536]{1,0:T(8,128)(2,1)S(1)} %copy-done, bf16[512,512]{1,0:T(8,128)(2,1)S(1)} %copy-done.2, ...), custom_call_target="tpu_custom_call" | custom-call | tf_op jit(solution)/shard_map/pallas_call | solution.py:335
  72.5 0.7 copy.10
Async XLA Ops:
  0.0 1.4 %copy-start = (bf16[512,1536]{1,0:T(8,128)(2,1)S(1)}, bf16[512,1536]{1,0:T(8,128)(2,1)}, u32[]{:S(2)}) copy-start(bf16[512,1536]{1,0:T(8,128)(2,1)} %w1_h.1) | copy-start | bytes 4718596
  1.4 1.4 %copy-start.1 = (bf16[512,1536]{1,0:T(8,128)(2,1)S(1)}, bf16[512,1536]{1,0:T(8,128)(2,1)}, u32[]{:S(2)}) copy-start(bf16[512,1536]{1,0:T(8,128)(2,1)} %w2_h.1) | copy-start | bytes 4718596
  2.8 1.0 %copy-start.2 = (bf16[512,512]{1,0:T(8,128)(2,1)S(1)}, bf16[512,512]{1,0:T(8,128)(2,1)}, u32[]{:S(2)}) copy-start(bf16[512,512]{1,0:T(8,128)(2,1)} %o1_h.1) | copy-start | bytes 1572868
  3.9 1.0 %copy-start.3 = (bf16[512,512]{1,0:T(8,128)(2,1)S(1)}, bf16[512,512]{1,0:T(8,128)(2,1)}, u32[]{:S(2)}) copy-start(bf16[512,512]{1,0:T(8,128)(2,1)} %o2_h.1) | copy-start | bytes 1572868
  4.9 0.9 %copy-start.4 = (bf16[2,128,512]{2,1,0:T(8,128)(2,1)S(1)}, bf16[2,128,512]{2,1,0:T(8,128)(2,1)}, u32[]{:S(2)}) copy-start(bf16[2,128,512]{2,1,0:T(8,128)(2,1)} %param.8) | copy-start | bytes 786436
  5.9 0.7 copy-start.5
  6.5 0.7 copy-start.6
  7.2 0.7 copy-start.7

commit v2 on v1

--- a/solution.py
+++ b/solution.py
@@ -100,8 +100,8 @@
             ((cnt_h, cnt), (dst_h, dst), (rot_h, rot), (pts_h, pts), (w1_h, w1), (o1_h, o1), (w2_h, w2), (o2_h, o2))
         )
     ]
-    for load in loads:
-        load.start()
+    for i in (3, 0, 1, 2, 4):
+        loads[i].start()
 
     def peer(dy, i):
         return ((x_me + i // 2) % NX) * (2 * NY) + ((y_me + dy) % NY) * 2 + (c_me + i) % 2
@@ -114,11 +114,8 @@
             for h in range(2):
                 j = 2 * g + h
 
-                def one(i, carry, j=j, g=g):
+                for i in range(1 if j == 0 else 0, 8):
                     visit(8 * j + i, g, DY[j], i)
-                    return carry
-
-                lax.fori_loop(1 if j == 0 else 0, 8, one, 0)
 
     barrier = pltpu.get_barrier_semaphore()
     up, down = (z + 1) % NZ, (z + NZ - 1) % NZ
@@ -168,6 +165,8 @@
                 sent.append(copy)
 
     ring(0)
+    for i in (5, 6, 7):
+        loads[i].start()
 
     loads[1].wait()
     loads[2].wait()
@@ -367,7 +366,7 @@
             dma((GROUPS,)),
         ],
         compiler_params=pltpu.CompilerParams(
-            collective_id=0, has_side_effects=True, vmem_limit_bytes=48 * 1024 * 1024
+            collective_id=0, has_side_effects=True, vmem_limit_bytes=64 * 1024 * 1024
         ),
     )(rows, counts, destination, rotated_ball, qkv_first, out_first, qkv_second, out_second)
     return result.reshape(points.shape)

time: 74 us -> 64.7 us (0.87)
  local copies, waits for them, and re-layouts: 8.59 us -> 1.67 us
  Pallas kernels: 64.6 us -> 62.1 us
    unnamed x17 -> x1, local copies, waits for them, and re-layouts: 8.59 us -> 1.67 us
    pallas_call x1, Pallas kernels: 64.6 us -> 62.1 us  [on_device(): pl.pallas_call(kernel, out_shape=jax.ShapeDtypeStruct((ROWS, WIDTH), BF16...]
where the time goes in v2:
time: 64.7 us; the launch traced here: 63.8 us
  Pallas kernels  62.1 us (96%)
  local copies, waits for them, and re-layouts  1.67 us (3%)
    pallas_call x1, Pallas kernels, on_device(): pl.pallas_call(kernel, out_shape=jax.ShapeDtypeStruct((ROWS, WIDTH), BF16...  62.1 us
    unnamed x1, local copies, waits for them, and re-layouts  1.67 us

profile of v2, /device:TPU:1, one launch (start us, length us, event | category | flops | bytes accessed | tf_op | source)
XLA Modules:
  0.0 63.8 jit_solution(2213942387928921416)
XLA Ops:
  0.0 62.1 %shard_map.82 = bf16[256,512]{1,0:T(8,128)(2,1)} custom-call(bf16[256,512]{1,0:T(8,128)(2,1)} %bitcast.3, s32[2,32]{1,0:T(2,128)} %cnt_h.1, s32[2,32]{1,0:T(2,128)} %dst_h.1, s32[2,32]{1,0:T(2,128)} %rot_h.1, bf16[512,1536]{1,0:T(8,128)(2,1)} %w1_h.1, bf16[512,512]{1,0:T(8,128)(2,1)} %o1_h.1, bf16[512,1536]{1,0:T(8,128)(2,1)} %w2_h.1, bf16[512,512]{1,0:T(8,128)(2,1)} %o2_h.1), custom_call_target="tpu_custom_call" | custom-call | tf_op jit(solution)/shard_map/pallas_call | solution.py:334
  62.2 1.7 %copy.10 = bf16[2,128,512]{2,1,0:T(8,128)(2,1)} copy(bf16[2,128,512]{2,1,0:T(8,128)(2,1)} %bitcast.2) | data formatting | bytes 524288

commit v3 on v2

--- a/solution.py
+++ b/solution.py
@@ -70,15 +70,28 @@
     return jnp.concatenate([jnp.where(low, pair, zero), jnp.where(low, zero, pair)], axis=0)
 
 
-def softmax_values(scores, values):
-    highest = jnp.max(scores, axis=1, keepdims=True)
-    weights = jnp.exp(scores - highest).astype(BF16)
-    ones = jnp.ones((values.shape[0], 128), BF16)
-    mixed = dot(weights, jnp.concatenate([values, ones], axis=1))
+def with_ones(values):
+    return jnp.concatenate([values, jnp.ones((values.shape[0], 128), BF16)], axis=1)
+
+
+def both_heads(mixed):
     mixed = mixed[:, :128] / mixed[:, 128:]
     half = mixed.shape[0] // 2
     low = iota((half, 128), 1) < 64
     return jnp.where(low, mixed[:half], mixed[half:])
+
+
+def softmax_part(scores, values):
+    highest = jnp.max(scores, axis=1, keepdims=True)
+    weights = jnp.exp(scores - highest).astype(BF16)
+    return highest, dot(weights, with_ones(values))
+
+
+def softmax_rest(part, scores, values):
+    before, mixed = part
+    highest = jnp.maximum(before, jnp.max(scores, axis=1, keepdims=True))
+    weights = jnp.exp(scores - highest).astype(BF16)
+    return both_heads(mixed * jnp.exp(before - highest) + dot(weights, with_ones(values)))
 
 
 def kernel(
@@ -94,13 +107,10 @@
     y_me = (wide // 2) % NY
     c_me = wide % 2
 
-    loads = [
-        pltpu.make_async_copy(src, dest, load_sem.at[i])
-        for i, (src, dest) in enumerate(
-            ((cnt_h, cnt), (dst_h, dst), (rot_h, rot), (pts_h, pts), (w1_h, w1), (o1_h, o1), (w2_h, w2), (o2_h, o2))
-        )
-    ]
-    for i in (3, 0, 1, 2, 4):
+    pairs = [(cnt_h, cnt), (dst_h, dst), (rot_h, rot), (w1_h, w1), (o1_h, o1), (w2_h, w2), (o2_h, o2)]
+    pairs += [(pts_h.at[pl.ds(b * SHARE, SHARE)], pts.at[pl.ds(b * SHARE, SHARE)]) for b in range(2)]
+    loads = [pltpu.make_async_copy(src, dest, load_sem.at[i]) for i, (src, dest) in enumerate(pairs)]
+    for i in (7, 0, 8, 1, 2, 3):
         loads[i].start()
 
     def peer(dy, i):
@@ -118,55 +128,53 @@
                     visit(8 * j + i, g, DY[j], i)
 
     barrier = pltpu.get_barrier_semaphore()
-    up, down = (z + 1) % NZ, (z + NZ - 1) % NZ
-    for other in (up, down):
-        pl.semaphore_signal(barrier, inc=1, device_id=(wide, other), device_id_type=MESH)
+    for away in (1, 7, 2, 6):
+        pl.semaphore_signal(barrier, inc=1, device_id=(wide, (z + away) % NZ), device_id_type=MESH)
 
     def greet(k, g, dy, i):
         pl.semaphore_signal(barrier, inc=1, device_id=(peer(dy, i), z), device_id_type=MESH)
 
     each_slot(greet)
 
-    loads[0].wait()
-    cnt64 = column(cnt, BLOCKS, 1)
-    r_b, r_l = iota((BLOCKS, ROWS), 0), iota((BLOCKS, ROWS), 1)
-    pool = (r_l // BLK == r_b) & ((r_l % BLK).astype(F32) < cnt64)
-    pool = jnp.where(pool, 1.0, 0.0).astype(BF16)
-    loads[3].wait()
-    normed_one = rms_round(pts[...].astype(F32))
-    pooled = (dot(pool, normed_one) / cnt64).astype(BF16)
-    ag[0] = pooled.reshape(2, BLOCKS // 2, WIDTH)
-
-    pl.semaphore_wait(barrier, WIDE - 1 + 2)
-
-    def hop(way, step, ball):
-        here = (step if way == 0 else (NZ - step) % NZ)
-        there = step + 1 if way == 0 else NZ - 1 - step
+    def hop(here, away, ball):
+        there = (here + away) % NZ
         return pltpu.make_async_remote_copy(
             src_ref=ag.at[here, ball],
             dst_ref=ag.at[there, ball],
-            send_sem=ring_send.at[way, step, ball],
+            send_sem=ring_send.at[there, ball],
             recv_sem=ring_recv.at[there, ball],
-            device_id=(wide, up if way == 0 else down),
+            device_id=(wide, (z + away) % NZ),
             device_id_type=MESH,
         )
 
+    def start(here, away, ball):
+        copy = hop(here, away, ball)
+        copy.start()
+        sent.append(copy)
+
     sent = []
-
-    def ring(step):
-        for ball in range(2):
-            for way in range(2):
-                if step == 3 and ball != way:
-                    continue
-                if step > 0:
-                    hop(way, step - 1, ball).wait_recv()
-                copy = hop(way, step, ball)
-                copy.start()
-                sent.append(copy)
-
-    ring(0)
-    for i in (5, 6, 7):
+    half = BLOCKS // 2
+    loads[0].wait()
+    cnt64 = column(cnt, BLOCKS, 1)
+    r_b, r_l = iota((half, SHARE), 0), iota((half, SHARE), 1)
+    normed = []
+    for ball in range(2):
+        count = cnt64[ball * half : (ball + 1) * half]
+        pool = (r_l // BLK == r_b) & ((r_l % BLK).astype(F32) < count)
+        pool = jnp.where(pool, 1.0, 0.0).astype(BF16)
+        loads[7 + ball].wait()
+        normed.append(rms_round(pts[ball * SHARE : (ball + 1) * SHARE, :].astype(F32)))
+        ag[0, ball] = (dot(pool, normed[ball]) / count).astype(BF16)
+        if ball == 0:
+            pl.semaphore_wait(barrier, WIDE - 1 + 4)
+        start(0, 2, ball)
+        start(0, 6, ball)
+    for ball in range(2):
+        start(0, 1, ball)
+        start(0, 7, ball)
+    for i in (4, 5, 6):
         loads[i].start()
+    normed_one = jnp.concatenate(normed, axis=0)
 
     loads[1].wait()
     loads[2].wait()
@@ -187,8 +195,6 @@
     unpack[...] = jnp.where(iota((ROWS, SLOTROWS), 1).astype(F32) == slot_col, 1.0, 0.0).astype(BF16)
     pack = jnp.where(iota((SLOTROWS, ROWS), 0).astype(F32) == slot_lane, 1.0, 0.0).astype(BF16)
 
-    ring(1)
-
     in_first = jnp.where(rot_col == 0.0, 1.0, 0.0)
     usable = jnp.where((iota((ROWS, 1), 0) % BLK).astype(F32) < cnt_col, 1.0, 0.0)
     lane = iota((ROWS, 128), 1)
@@ -213,44 +219,68 @@
     def send_meta(k, g, dy, i):
         move(meta_s, meta_r, k, meta_send, meta_recv, peer(dy, i)).start()
 
+    bias = jnp.where(to_lanes(usable) > 0.0, 0.0, NEGATIVE)
+    loads[3].wait()
+    qkv1[...] = dot(normed_one, w1[...]).astype(BF16)
+
+    for ball in range(2):
+        hop(0, 2, ball).wait_recv()
+        start(2, 1, ball)
+        if ball == 0:
+            start(2, 2, ball)
+        hop(0, 6, ball).wait_recv()
+        start(6, 7, ball)
+        if ball == 1:
+            start(6, 6, ball)
+
     each_slot(send_meta)
 
-    loads[4].wait()
-    qkv1[...] = dot(normed_one, w1[...]).astype(BF16)
-    ring(2)
-    bias = jnp.where(to_lanes(usable) > 0.0, 0.0, NEGATIVE)
-    ring(3)
-    for ball in range(2):
-        hop(0, 2, 1 - ball).wait_recv() if ball == 0 else hop(1, 2, 1 - ball).wait_recv()
-    hop(0, 3, 0).wait_recv()
-    hop(1, 3, 1).wait_recv()
-
-    attended = []
-    for ball in range(2):
-        pooled_all = ag[:, ball].reshape(NZ * BLOCKS // 2, WIDTH)
-        pooled_kv = dot(pooled_all, w1[:, WIDTH:]).astype(BF16)
+    for ball in range(2):
+        hop(0, 1, ball).wait_recv()
+        hop(0, 7, ball).wait_recv()
+    near = [ag[d, ball] for ball in range(2) for d in (0, 1, 2, 7)]
+    near_kv = dot(jnp.concatenate(near, axis=0), w1[:, WIDTH:]).astype(BF16)
+    queries, begun = [], []
+    for ball in range(2):
         mine = pl.ds(ball * SHARE, SHARE)
+        rows = slice(ball * 4 * half, (ball + 1) * 4 * half)
         bias_ball = jnp.concatenate(
-            [bias[:, ball * SHARE : (ball + 1) * SHARE], jnp.zeros((1, NZ * BLOCKS // 2), F32)], axis=1
+            [bias[:, ball * SHARE : (ball + 1) * SHARE], jnp.zeros((1, 4 * half), F32)], axis=1
         )
-        parts = []
         for pair in range(PAIRS):
             at = pair * 128
             query = two_heads(qkv1[mine, at : at + 128] * 0.125)
             key = jnp.concatenate(
-                [qkv1[mine, WIDTH + at : WIDTH + at + 128], pooled_kv[:, at : at + 128]], axis=0
+                [qkv1[mine, WIDTH + at : WIDTH + at + 128], near_kv[rows, at : at + 128]], axis=0
             )
             value = jnp.concatenate(
                 [
                     qkv1[mine, 2 * WIDTH + at : 2 * WIDTH + at + 128],
-                    pooled_kv[:, WIDTH + at : WIDTH + at + 128],
+                    near_kv[rows, WIDTH + at : WIDTH + at + 128],
                 ],
                 axis=0,
             )
-            parts.append(softmax_values(dot_t(query, key) + bias_ball, value).astype(BF16))
+            queries.append(query)
+            begun.append(softmax_part(dot_t(query, key) + bias_ball, value))
+    for ball in range(2):
+        hop(2, 1, ball).wait_recv()
+        hop(6, 7, ball).wait_recv()
+    hop(2, 2, 0).wait_recv()
+    hop(6, 6, 1).wait_recv()
+    far = [ag[d, ball] for ball in range(2) for d in (3, 4, 5, 6)]
+    far_kv = dot(jnp.concatenate(far, axis=0), w1[:, WIDTH:]).astype(BF16)
+    attended = []
+    for ball in range(2):
+        rows = slice(ball * 4 * half, (ball + 1) * 4 * half)
+        parts = []
+        for pair in range(PAIRS):
+            at = pair * 128
+            key, value = far_kv[rows, at : at + 128], far_kv[rows, WIDTH + at : WIDTH + at + 128]
+            scores = dot_t(queries[ball * PAIRS + pair], key)
+            parts.append(softmax_rest(begun[ball * PAIRS + pair], scores, value).astype(BF16))
         attended.append(jnp.concatenate(parts, axis=1))
     attended_one = jnp.concatenate(attended, axis=0)
-    loads[5].wait()
+    loads[4].wait()
     layer_one = (pts[...].astype(F32) + dot(attended_one, o1[...])).astype(BF16)
     pts[...] = layer_one
     normed_two = rms_round(layer_one.astype(F32))
@@ -283,7 +313,7 @@
     query_mark = jnp.where(use, pltpu.roll(marks, 2, 1), 0.0).astype(BF16)
     key_mark = jnp.where(use, (1.0 - marks) * NEGATIVE, 0.0).astype(BF16)
 
-    loads[6].wait()
+    loads[5].wait()
     for g in range(GROUPS):
         first, count = group(g)
         arrived(snd, rcv, first, count, fwd_send, fwd_recv.at[g]).wait_recv()
@@ -300,7 +330,7 @@
             query = jnp.concatenate([query, jnp.concatenate([mark, mark], axis=0)], axis=1)
             key = jnp.concatenate([qkv2[:, WIDTH + at : WIDTH + at + 128], key_mark], axis=1)
             value = qkv2[:, 2 * WIDTH + at : 2 * WIDTH + at + 128]
-            parts.append(softmax_values(dot_t(query, key), value))
+            parts.append(both_heads(softmax_part(dot_t(query, key), value)[1]))
         mixture = jnp.concatenate(parts, axis=1).reshape(GSLOTS, SLOT, WIDTH).astype(BF16)
         bsnd[g * GSLOTS : (g + 1) * GSLOTS] = mixture
         if g == 0:
@@ -311,7 +341,7 @@
 
         each_slot(send_back, (g,))
 
-    loads[7].wait()
+    loads[6].wait()
     total = jnp.zeros((ROWS, WIDTH), F32)
     for g in range(GROUPS):
         first, count = group(g)
@@ -355,8 +385,8 @@
             pltpu.VMEM((ROWS, 3 * WIDTH), BF16),
             pltpu.VMEM((SLOTROWS, 3 * WIDTH), BF16),
             pltpu.VMEM((ROWS, SLOTROWS), BF16),
-            dma((8,)),
-            dma((2, 4, 2)),
+            dma((9,)),
+            dma((NZ, 2)),
             dma((NZ, 2)),
             dma,
             dma,
@@ -366,9 +396,9 @@
             dma((GROUPS,)),
         ],
         compiler_params=pltpu.CompilerParams(
-            collective_id=0, has_side_effects=True, vmem_limit_bytes=64 * 1024 * 1024
+            collective_id=0, has_side_effects=True, vmem_limit_bytes=48 * 1024 * 1024
         ),
-    )(rows, counts, destination, rotated_ball, qkv_first, out_first, qkv_second, out_second)
+    )(*[pltpu.with_memory_space_constraint(a, pltpu.HBM) for a in (rows, counts, destination, rotated_ball, qkv_first, out_first, qkv_second, out_second)])
     return result.reshape(points.shape)
 
 

time: 64.7 us -> 62 us (0.958)
  Pallas kernels: 62.1 us -> 60.3 us
  local copies, waits for them, and re-layouts: 1.67 us -> 0.71 us
    pallas_call x1, Pallas kernels: 62.1 us -> 60.3 us  [on_device(): pl.pallas_call(kernel, out_shape=jax.ShapeDtypeStruct((ROWS, WIDTH), BF16...]
    unnamed x1, local copies, waits for them, and re-layouts: 1.67 us -> 0.71 us
where the time goes in v3:
time: 62 us; the launch traced here: 61 us
  Pallas kernels  60.3 us (97%)
  local copies, waits for them, and re-layouts  0.71 us (1%)
    pallas_call x1, Pallas kernels, on_device(): pl.pallas_call(kernel, out_shape=jax.ShapeDtypeStruct((ROWS, WIDTH), BF16...  60.3 us

profile of v3, /device:TPU:1, one launch (start us, length us, event | category | flops | bytes accessed | tf_op | source)
XLA Modules:
  0.0 61.0 jit_solution(16226525853114544067)
XLA Ops:
  0.0 60.3 %shard_map.82 = bf16[256,512]{1,0:T(8,128)(2,1)S(1)} custom-call(bf16[256,512]{1,0:T(8,128)(2,1)} %bitcast.3, s32[2,32]{1,0:T(2,128)} %cnt_h.1, s32[2,32]{1,0:T(2,128)} %dst_h.1, s32[2,32]{1,0:T(2,128)} %rot_h.1, bf16[512,1536]{1,0:T(8,128)(2,1)} %w1_h.1, bf16[512,512]{1,0:T(8,128)(2,1)} %o1_h.1, bf16[512,1536]{1,0:T(8,128)(2,1)} %w2_h.1, bf16[512,512]{1,0:T(8,128)(2,1)} %o2_h.1), custom_call_target="tpu_custom_call" | custom-call | tf_op jit(solution)/shard_map/pallas_call | solution.py:364
  60.3 0.7 %copy.10 = bf16[2,128,512]{2,1,0:T(8,128)(2,1)} copy(bf16[2,128,512]{2,1,0:T(8,128)(2,1)S(1)} %bitcast.2) | data formatting | bytes 524288

commit v4 on v3

--- a/solution.py
+++ b/solution.py
@@ -119,13 +119,10 @@
     def source(dy, i):
         return ((x_me + NX - i // 2) % NX) * (2 * NY) + ((y_me + NY - dy) % NY) * 2 + (c_me + i) % 2
 
-    def each_slot(visit, groups=range(GROUPS)):
-        for g in groups:
-            for h in range(2):
-                j = 2 * g + h
-
-                for i in range(1 if j == 0 else 0, 8):
-                    visit(8 * j + i, g, DY[j], i)
+    def each_slot(visit, groups=range(GROUPS), order=None):
+        for j, i in order or [(j, i) for j in range(8) for i in range(8)]:
+            if (j, i) != (0, 0) and j // 2 in groups:
+                visit(8 * j + i, j // 2, DY[j], i)
 
     barrier = pltpu.get_barrier_semaphore()
     for away in (1, 7, 2, 6):
@@ -291,7 +288,7 @@
     def send_rows(k, g, dy, i):
         move(snd, rcv, k, fwd_send, fwd_recv.at[g], peer(dy, i)).start()
 
-    each_slot(send_rows)
+    each_slot(send_rows, order=[(j, i) for j in range(8) for i in (4, 5, 2, 6, 3, 7, 0, 1)])
 
     def arrived(src, dest, first, count, send_sem, recv_sem):
         return pltpu.make_async_remote_copy(
@@ -314,23 +311,34 @@
     key_mark = jnp.where(use, (1.0 - marks) * NEGATIVE, 0.0).astype(BF16)
 
     loads[5].wait()
-    for g in range(GROUPS):
+    def project(g):
         first, count = group(g)
         arrived(snd, rcv, first, count, fwd_send, fwd_recv.at[g]).wait_recv()
         rows = rcv[g * GSLOTS : (g + 1) * GSLOTS].astype(F32).reshape(GROWS, WIDTH).astype(BF16)
         qkv2[g * GROWS : (g + 1) * GROWS, :] = dot(rows, w2[...]).astype(BF16)
 
+    def scored(g, pair, keys):
+        at = pair * 128
+        mark = query_mark[g * GROWS : (g + 1) * GROWS]
+        query = two_heads(qkv2[g * GROWS : (g + 1) * GROWS, at : at + 128] * 0.125)
+        query = jnp.concatenate([query, jnp.concatenate([mark, mark], axis=0)], axis=1)
+        key = jnp.concatenate([qkv2[keys, WIDTH + at : WIDTH + at + 128], key_mark[keys]], axis=1)
+        return dot_t(query, key), qkv2[keys, 2 * WIDTH + at : 2 * WIDTH + at + 128]
+
+    last = GROUPS - 1
+    early, late = slice(0, last * GROWS), slice(last * GROWS, SLOTROWS)
+    for g in range(last):
+        project(g)
+    begun_two = [[softmax_part(*scored(g, pair, early)) for pair in range(PAIRS)] for g in range(1)]
+    project(last)
+
     for g in range(GROUPS):
-        mine = slice(g * GROWS, (g + 1) * GROWS)
-        mark = query_mark[mine]
         parts = []
         for pair in range(PAIRS):
-            at = pair * 128
-            query = two_heads(qkv2[mine, at : at + 128] * 0.125)
-            query = jnp.concatenate([query, jnp.concatenate([mark, mark], axis=0)], axis=1)
-            key = jnp.concatenate([qkv2[:, WIDTH + at : WIDTH + at + 128], key_mark], axis=1)
-            value = qkv2[:, 2 * WIDTH + at : 2 * WIDTH + at + 128]
-            parts.append(both_heads(softmax_part(dot_t(query, key), value)[1]))
+            if g < 1:
+                parts.append(softmax_rest(begun_two[g][pair], *scored(g, pair, late)))
+            else:
+                parts.append(both_heads(softmax_part(*scored(g, pair, slice(0, SLOTROWS)))[1]))
         mixture = jnp.concatenate(parts, axis=1).reshape(GSLOTS, SLOT, WIDTH).astype(BF16)
         bsnd[g * GSLOTS : (g + 1) * GSLOTS] = mixture
         if g == 0:
@@ -339,7 +347,7 @@
         def send_back(k, g, dy, i):
             move(bsnd, brcv, k, back_send, back_recv.at[g], source(dy, i)).start()
 
-        each_slot(send_back, (g,))
+        each_slot(send_back, (g,), [(j, i) for j in range(8) for i in (4, 5, 2, 6, 3, 7, 0, 1)])
 
     loads[6].wait()
     total = jnp.zeros((ROWS, WIDTH), F32)

time: 62 us -> 60.2 us (0.971); the launches traced: 61 us -> 59.9 us
  Pallas kernels: 60.3 us -> 59.2 us
    pallas_call x1, Pallas kernels: 60.3 us -> 59.2 us  [on_device(): pl.pallas_call(kernel, out_shape=jax.ShapeDtypeStruct((ROWS, WIDTH), BF16...]
where the time goes in v4:
time: 60.2 us; the launch traced here: 59.9 us
  Pallas kernels  59.2 us (98%)
  local copies, waits for them, and re-layouts  0.71 us (1%)
    pallas_call x1, Pallas kernels, on_device(): pl.pallas_call(kernel, out_shape=jax.ShapeDtypeStruct((ROWS, WIDTH), BF16...  59.2 us

profile of v4, /device:TPU:1, one launch (start us, length us, event | category | flops | bytes accessed | tf_op | source)
XLA Modules:
  0.0 59.9 jit_solution(17815324036510386620)
XLA Ops:
  0.0 59.2 %shard_map.82 = bf16[256,512]{1,0:T(8,128)(2,1)S(1)} custom-call(bf16[256,512]{1,0:T(8,128)(2,1)} %bitcast.3, s32[2,32]{1,0:T(2,128)} %cnt_h.1, s32[2,32]{1,0:T(2,128)} %dst_h.1, s32[2,32]{1,0:T(2,128)} %rot_h.1, bf16[512,1536]{1,0:T(8,128)(2,1)} %w1_h.1, bf16[512,512]{1,0:T(8,128)(2,1)} %o1_h.1, bf16[512,1536]{1,0:T(8,128)(2,1)} %w2_h.1, bf16[512,512]{1,0:T(8,128)(2,1)} %o2_h.1), custom_call_target="tpu_custom_call" | custom-call | tf_op jit(solution)/shard_map/pallas_call | solution.py:372
  59.2 0.7 %copy.10 = bf16[2,128,512]{2,1,0:T(8,128)(2,1)} copy(bf16[2,128,512]{2,1,0:T(8,128)(2,1)S(1)} %bitcast.2) | data formatting | bytes 524288

commit v5 on v4

--- a/solution.py
+++ b/solution.py
@@ -329,13 +329,13 @@
     early, late = slice(0, last * GROWS), slice(last * GROWS, SLOTROWS)
     for g in range(last):
         project(g)
-    begun_two = [[softmax_part(*scored(g, pair, early)) for pair in range(PAIRS)] for g in range(1)]
+    begun_two = [[softmax_part(*scored(g, pair, early)) for pair in range(PAIRS)] for g in range(2)]
     project(last)
 
     for g in range(GROUPS):
         parts = []
         for pair in range(PAIRS):
-            if g < 1:
+            if g < 2:
                 parts.append(softmax_rest(begun_two[g][pair], *scored(g, pair, late)))
             else:
                 parts.append(both_heads(softmax_part(*scored(g, pair, slice(0, SLOTROWS)))[1]))

time: 60.2 us -> 60.3 us (level)
  no operation moved by 1% of the time
where the time goes in v5:
time: 60.3 us; the launch traced here: 59.6 us
  Pallas kernels  58.9 us (98%)
  local copies, waits for them, and re-layouts  0.71 us (1%)
    pallas_call x1, Pallas kernels, on_device(): pl.pallas_call(kernel, out_shape=jax.ShapeDtypeStruct((ROWS, WIDTH), BF16...  58.9 us

profile of v5, /device:TPU:1, one launch (start us, length us, event | category | flops | bytes accessed | tf_op | source)
XLA Modules:
  0.0 59.6 jit_solution(10932133758564506126)
XLA Ops:
  0.0 58.9 %shard_map.82 = bf16[256,512]{1,0:T(8,128)(2,1)S(1)} custom-call(bf16[256,512]{1,0:T(8,128)(2,1)} %bitcast.3, s32[2,32]{1,0:T(2,128)} %cnt_h.1, s32[2,32]{1,0:T(2,128)} %dst_h.1, s32[2,32]{1,0:T(2,128)} %rot_h.1, bf16[512,1536]{1,0:T(8,128)(2,1)} %w1_h.1, bf16[512,512]{1,0:T(8,128)(2,1)} %o1_h.1, bf16[512,1536]{1,0:T(8,128)(2,1)} %w2_h.1, bf16[512,512]{1,0:T(8,128)(2,1)} %o2_h.1), custom_call_target="tpu_custom_call" | custom-call | tf_op jit(solution)/shard_map/pallas_call | solution.py:372
  58.9 0.7 %copy.10 = bf16[2,128,512]{2,1,0:T(8,128)(2,1)} copy(bf16[2,128,512]{2,1,0:T(8,128)(2,1)S(1)} %bitcast.2) | data formatting | bytes 524288
